TPU v7x, 32 devices: a whole 2x2x4 slice. The times are simulated.
32 devices in a mesh: peer: 8 (over z, y), grp: 4 (over x, core).
Axes of the slice: x: 2, y: 2, z: 4, core: 2. Of those that a mesh axis runs over, the one named last changes fastest.
Arguments:
- tokens: bfloat16 [4096, 2048], P(('peer', 'grp')), may hold values from -6 to 6
- cotangent: bfloat16 [4096, 2048], P(('peer', 'grp')), may hold values from -6 to 6
- expert_ids: int32 [4096, 4], P(('peer', 'grp')), may hold values from 0 to 31, all different within a row; in each aligned block of 128 rows (0 to 127, 128 to 255, ...) at most 32 rows name the same one
- route_prob: float32 [4096, 4], P(('peer', 'grp')), may hold values from 0.1 to 1
- w_gate: bfloat16 [8, 2048, 704], P('peer', None, 'grp'), may hold values from -0.125 to 0.125
- w_up: bfloat16 [8, 2048, 704], P('peer', None, 'grp'), may hold values from -0.125 to 0.125
- w_down: bfloat16 [8, 704, 2048], P('peer', 'grp'), may hold values from -0.21875 to 0.21875
- student_logits: bfloat16 [8, 8, 151936], P('peer', None, 'grp'), may hold values from -24 to 252
- stale_logits: bfloat16 [8, 8, 151936], P('peer', None, 'grp'), may hold values from -24 to 252
- labels: int32 [8, 8], P('peer'), may hold values from 0 to 151935
Outputs:
- layer_out: bfloat16 [4096, 2048], P(('peer', 'grp'))
- input_grad: bfloat16 [4096, 2048], P(('peer', 'grp'))
- prob_grad: float32 [4096, 4], P(('peer', 'grp'))
- distill_loss: float32 [8, 8], P('peer')
- logit_grad: bfloat16 [8, 8, 151936], P('peer', None, 'grp')
Inputs may be any that keep to these rules, and one draw needn't show every extreme that they name: `expert_ids`: each row names 4 different experts; the rows of one device name any one expert at most 32 times.
All inputs are finite; a program needn't handle non-finite values.
Results may differ from a plain program's by a relative error of at most 0.0064.
Values may be sent and summed in bfloat16 or wider, within the bound.
No kernel may reach another device: no remote copies, remote signals or barrier semaphores. Data moves between devices by JAX's collectives and lax.ppermute only.
A program may use at most 64 MiB of HBM per device.

v0:
```python
import jax
import jax.numpy as jnp
from jax import lax
from jax.sharding import PartitionSpec as P

PIECES = 4
CAP = 32


def joined(value, axis, combine):
    everything = jax.tree.map(lambda part: lax.all_gather(part, axis), value)
    leading = jax.tree.map(lambda part: part[0], everything)

    def lap(k, so_far):
        return combine(so_far, jax.tree.map(lambda part: part[k], everything))

    return lax.fori_loop(1, lax.axis_size(axis), lap, leading)


def from_behind(value, axis, steps):
    count = lax.axis_size(axis)
    pairs = [(source, (source + steps) % count) for source in range(count)]
    return lax.ppermute(value, axis, pairs)


def slot_tables(expert_ids, n_window, capacity):
    window_iota = lax.broadcasted_iota(jnp.int32, (1, 1, n_window), 2)
    member = jnp.sum((expert_ids[:, :, None] == window_iota).astype(jnp.int32), axis=1)
    position = jnp.cumsum(member, axis=0) - member
    slot_iota = lax.broadcasted_iota(jnp.int32, (1, capacity, 1), 1)
    select = (position.T[:, None, :] == slot_iota) & (member.T[:, None, :] > 0)
    return (position, select)


def forward_piece(slot_rows, gate_cols, up_cols, down_rows):
    gate_act = jnp.dot(slot_rows, gate_cols, preferred_element_type=jnp.float32)
    up_act = jnp.dot(slot_rows, up_cols, preferred_element_type=jnp.float32)
    hidden = (gate_act * jax.nn.sigmoid(gate_act) * up_act).astype(jnp.bfloat16)
    piece_out = jnp.dot(hidden, down_rows, preferred_element_type=jnp.float32).astype(jnp.bfloat16)
    return (piece_out, gate_act, up_act)


def backward_piece(scaled_rows, gate_act, up_act, gate_cols, up_cols, down_rows):
    contract = (((1,), (1,)), ((), ()))
    grad_hidden = lax.dot_general(
        scaled_rows, down_rows, contract, preferred_element_type=jnp.float32
    )
    sigmoid_gate = jax.nn.sigmoid(gate_act)
    grad_gate = (
        grad_hidden * up_act * sigmoid_gate * (1.0 + gate_act * (1.0 - sigmoid_gate))
    ).astype(jnp.bfloat16)
    grad_up = (grad_hidden * gate_act * sigmoid_gate).astype(jnp.bfloat16)
    piece_grad = lax.dot_general(grad_gate, gate_cols, contract, preferred_element_type=jnp.float32)
    piece_grad = piece_grad + lax.dot_general(
        grad_up, up_cols, contract, preferred_element_type=jnp.float32
    )
    return piece_grad.astype(jnp.bfloat16)


def join_stats(first_side, second_side):
    max_one, sum_one, tmax_one, tsum_one, cross_one, label_one = first_side
    max_two, sum_two, tmax_two, tsum_two, cross_two, label_two = second_side
    max_both = jnp.maximum(max_one, max_two)
    tmax_both = jnp.maximum(tmax_one, tmax_two)
    scale_one = jnp.exp(tmax_one - tmax_both)
    scale_two = jnp.exp(tmax_two - tmax_both)
    sum_both = sum_one * jnp.exp(max_one - max_both) + sum_two * jnp.exp(max_two - max_both)
    tsum_both = tsum_one * scale_one + tsum_two * scale_two
    cross_both = cross_one * scale_one + cross_two * scale_two
    return (max_both, sum_both, tmax_both, tsum_both, cross_both, label_one + label_two)


def distill(student_logits, teacher_now, labels):
    student = student_logits[0].astype(jnp.float32)
    teacher = teacher_now[0].astype(jnp.float32)
    shard_width = student.shape[1]
    vocab_ids = lax.axis_index("grp") * shard_width + lax.broadcasted_iota(
        jnp.int32, student.shape, 1
    )
    label_hit = vocab_ids == labels[0][:, None]
    label_logit = jnp.sum(jnp.where(label_hit, student, 0.0), axis=1)
    local_smax = jnp.max(student, axis=1)
    local_tmax = jnp.max(teacher, axis=1)
    student_exp = jnp.sum(jnp.exp(student - local_smax[:, None]), axis=1)
    teacher_exp = jnp.exp(teacher - local_tmax[:, None])
    teacher_sum = jnp.sum(teacher_exp, axis=1)
    cross_sum = jnp.sum(teacher_exp * (teacher - student), axis=1)
    max_student, student_sum, max_teacher, teacher_sum, cross_sum, label_logit = joined(
        (local_smax, student_exp, local_tmax, teacher_sum, cross_sum, label_logit),
        "grp",
        join_stats,
    )
    lse_student = max_student + jnp.log(student_sum)
    lse_teacher = max_teacher + jnp.log(teacher_sum)
    distill_loss = 2.0 * lse_student - label_logit + cross_sum / teacher_sum - lse_teacher
    teacher_prob = jnp.exp(teacher - lse_teacher[:, None])
    logit_grad = (
        2.0 * jnp.exp(student - lse_student[:, None]) - label_hit.astype(jnp.float32) - teacher_prob
    ).astype(jnp.bfloat16)
    return (distill_loss[None], logit_grad[None])


def body(
    tokens,
    cotangent,
    expert_ids,
    route_prob,
    w_gate,
    w_up,
    w_down,
    student_logits,
    stale_logits,
    labels,
):
    group_size = lax.axis_size("grp")
    n_window = group_size // PIECES
    gate_cols = w_gate[0]
    up_cols = w_up[0]
    down_rows = w_down[0]
    model_width = tokens.shape[1]
    half_cap = CAP // 2
    position, select = slot_tables(expert_ids, n_window, CAP)
    select_bf = select.astype(jnp.bfloat16)
    window_iota = lax.broadcasted_iota(jnp.int32, (1, 1, n_window), 2)
    token_prob = jnp.sum(
        route_prob[:, :, None] * (expert_ids[:, :, None] == window_iota).astype(jnp.float32), axis=1
    )
    slot_prob = jnp.einsum(
        "ect,te->ec", select.astype(jnp.float32), token_prob, precision=lax.Precision.HIGHEST
    )
    slot_rows = jnp.einsum(
        "ect,td->ecd", select_bf, tokens, preferred_element_type=jnp.float32
    ).astype(jnp.bfloat16)
    slot_cot = jnp.einsum("ect,td->ecd", select_bf, cotangent, preferred_element_type=jnp.float32)
    slot_scaled = (slot_prob[:, :, None] * slot_cot).astype(jnp.bfloat16)
    send_rows = jnp.repeat(slot_rows, PIECES, axis=0).reshape(group_size, 2, half_cap, model_width)
    send_scaled = jnp.repeat(slot_scaled, PIECES, axis=0).reshape(
        group_size, 2, half_cap, model_width
    )
    recv_rows = lax.all_to_all(send_rows, "grp", split_axis=0, concat_axis=0, tiled=True)
    recv_scaled = lax.all_to_all(send_scaled, "grp", split_axis=0, concat_axis=0, tiled=True)
    item_count = recv_rows.shape[1]
    flat_rows = recv_rows.reshape(-1, model_width)
    flat_scaled = recv_scaled.reshape(-1, model_width)
    piece_out, gate_act, up_act = forward_piece(flat_rows, gate_cols, up_cols, down_rows)
    piece_out = piece_out.reshape(group_size, item_count, half_cap, model_width)
    piece_grad = backward_piece(flat_scaled, gate_act, up_act, gate_cols, up_cols, down_rows)
    piece_grad = piece_grad.reshape(group_size, item_count, half_cap, model_width)
    back_out = lax.all_to_all(piece_out, "grp", split_axis=0, concat_axis=0, tiled=True)
    back_grad = lax.all_to_all(piece_grad, "grp", split_axis=0, concat_axis=0, tiled=True)
    back_out, back_grad = (back_out, back_grad)
    expert_out = jnp.sum(
        back_out.astype(jnp.float32).reshape(n_window, PIECES, CAP, model_width), axis=1
    )
    expert_grad = jnp.sum(
        back_grad.astype(jnp.float32).reshape(n_window, PIECES, CAP, model_width), axis=1
    )
    in_window = expert_ids < n_window
    safe_ids = jnp.where(in_window, expert_ids, 0)
    slot_index = jnp.take_along_axis(position, safe_ids, axis=1)
    flat_index = safe_ids * CAP + slot_index
    out_rows = jnp.where(
        in_window[:, :, None],
        jnp.take(expert_out.reshape(-1, model_width), flat_index, axis=0),
        0.0,
    )
    grad_rows = jnp.where(
        in_window[:, :, None],
        jnp.take(expert_grad.reshape(-1, model_width), flat_index, axis=0),
        0.0,
    )
    layer_out = jnp.sum(route_prob[:, :, None] * out_rows, axis=1).astype(jnp.bfloat16)
    prob_grad = jnp.sum(cotangent.astype(jnp.float32)[:, None, :] * out_rows, axis=2)
    input_grad = jnp.sum(grad_rows, axis=1).astype(jnp.bfloat16)
    teacher_now = from_behind(stale_logits, "peer", 1)
    distill_loss, logit_grad = distill(student_logits, teacher_now, labels)
    return (layer_out, input_grad, prob_grad, distill_loss, logit_grad)


def solution(mesh):
    placed = (
        P(("peer", "grp"), None),
        P(("peer", "grp"), None),
        P(("peer", "grp"), None),
        P(("peer", "grp"), None),
        P("peer", None, "grp"),
        P("peer", None, "grp"),
        P("peer", "grp", None),
        P("peer", None, "grp"),
        P("peer", None, "grp"),
        P("peer", None),
    )
    return jax.shard_map(
        body,
        mesh=mesh,
        in_specs=placed,
        out_specs=(
            P(("peer", "grp"), None),
            P(("peer", "grp"), None),
            P(("peer", "grp"), None),
            P("peer", None),
            P("peer", None, "grp"),
        ),
        check_vma=False,
    )
```

profile of v0, /device:TPU:0, one launch (start us, length us, event | category | flops | bytes accessed | tf_op | source)
XLA Modules:
  0.0 88.1 jit_solution(13793682521302028346)
XLA Ops:
  0.6 3.0 %collective-permute-start = (bf16[1,8,37984]{2,1,0:T(8,128)(2,1)}, bf16[1,8,37984]{2,1,0:T(8,128)(2,1)S(1)}, u32[]{:S(2)}, u32[]{:S(2)}) collective-permute-start(bf16[1,8,37984]{2,1,0:T(8,128)(2,1)} %param.22), channel_id=1, source_target_pairs={{0,4},{4,8},{8,12},{12,16},{16,20},{20,24},{24,28},{28,0},{1,5},{5... | collective-permute-start | bytes 1823240 | tf_op jit(solution)/shard_map/ppermute | solution.py:23
  3.7 0.7 select_reduce_fusion
  4.9 1.2 %convolution_convert_fusion.1 = bf16[32,2048]{1,0:T(8,128)(2,1)S(1)} fusion(bf16[128,2048]{1,0:T(8,128)(2,1)} %param.14, s32[128]{0:T(128)S(1)} %sub.111, pred[128]{0:T(512)(128)(4,1)S(1)} %broadcast_compare_fusion.2), kind=kOutput, calls=%fused_computation.36 | convolution fusion | flops 16850944 | bytes 656000 | tf_op jit(solution)/shard_map/ect,td->ecd/dot_general | solution.py:131
  6.1 0.8 broadcast_in_dim.63
  7.0 3.5 %all-to-all-start = ((bf16[4,2,16,2048]{3,2,1,0:T(8,128)(2,1)}), bf16[4,2,16,2048]{3,2,1,0:T(8,128)(2,1)S(1)}, u32[]{:S(2)}, u32[]{:S(2)}) async-start(bf16[4,2,16,2048]{3,2,1,0:T(8,128)(2,1)} %broadcast_in_dim.63), calls=%async_computation | async-start | bytes 1048576 | tf_op jit(solution)/shard_map/all_to_all | solution.py:140
  10.8 3.4 %gather_fusion = s32[512]{0:T(512)S(1)} fusion(s32[128,1]{1,0:T(8,128)S(1)} %get-tuple-element.386, s32[512]{0:T(512)S(1)} %reshape.285), kind=kCustom, calls=%fused_computation.2 | custom fusion | bytes 8192 | tf_op jit(solution)/shard_map/jit(take_along_axis)/gather | solution.py:160
  14.6 0.4 reduce_max.36
  15.1 0.6 dynamic-slice
  16.4 0.7 copy.40
  17.5 1.2 %convert_element_type.89 = f32[128,2048]{1,0:T(8,128)} convert(bf16[128,2048]{1,0:T(8,128)(2,1)S(1)} %copy-done.5) | non-fusion elementwise | flops 262144 | bytes 1572864 | tf_op jit(solution)/shard_map/convert_element_type | solution.py:173
  19.2 0.8 broadcast_in_dim.67
  20.1 4.3 %all-to-all-start.2 = ((bf16[4,2,16,2048]{3,2,1,0:T(8,128)(2,1)}), bf16[4,2,16,2048]{3,2,1,0:T(8,128)(2,1)}, u32[]{:S(2)}, u32[]{:S(2)}) async-start(bf16[4,2,16,2048]{3,2,1,0:T(8,128)(2,1)} %broadcast_in_dim.67), calls=%async_computation.2 | async-start | bytes 1048576 | tf_op jit(solution)/shard_map/all_to_all | solution.py:141
  24.3 0.4 fusion.43
  24.7 1.0 %fusion.39 = f32[128,176]{0,1:T(8,128)} fusion(bf16[128,2048]{1,0:T(8,128)(2,1)S(1)} %bitcast.127, bf16[1,2048,176]{1,2,0:T(8,128)(2,1)S(1)} %copy-done.3), kind=kOutput, calls=%fused_computation.65 | convolution fusion | flops 92274688 | bytes 1335296 | tf_op jit(solution)/shard_map/dot_general | solution.py:37
  25.8 7.4 %all-to-all-done.2 = bf16[4,2,16,2048]{3,2,1,0:T(8,128)(2,1)} async-done(((bf16[4,2,16,2048]{3,2,1,0:T(8,128)(2,1)}), bf16[4,2,16,2048]{3,2,1,0:T(8,128)(2,1)}, u32[]{:S(2)}, u32[]{:S(2)}) %all-to-all-start.2) | async-done | bytes 524320 | tf_op jit(solution)/shard_map/all_to_all | solution.py:141
  33.2 1.6 %fusion.35 = f32[128,176]{0,1:T(8,128)S(1)} fusion(bf16[128,2048]{1,0:T(8,128)(2,1)} %bitcast.18, bf16[1,176,2048]{2,1,0:T(8,128)(2,1)} %param.20), kind=kOutput, calls=%fused_computation.61 | convolution fusion | flops 92274688 | bytes 1335296 | tf_op jit(solution)/shard_map/dot_general | solution.py:45
  34.8 0.4 fusion.41
  35.2 1.1 %fusion.16 = bf16[128,2048]{1,0:T(8,128)(2,1)} fusion(f32[128,2048]{1,0:T(8,128)S(1)} %fusion.41, bf16[1,2048,176]{1,2,0:T(8,128)(2,1)S(1)} %copy-done.3, f32[128,176]{0,1:T(8,128)S(1)} %fusion.35, f32[128,176]{0,1:T(8,128)S(1)} %fusion.43), kind=kOutput, calls=%fused_computation.32 | convolution fusion | flops 92934144 | bytes 2473984 | tf_op jit(solution)/shard_map/dot_general | solution.py:54
  36.4 3.6 %all-to-all-start.3 = ((bf16[4,2,16,2048]{3,2,1,0:T(8,128)(2,1)}), bf16[4,2,16,2048]{3,2,1,0:T(8,128)(2,1)S(1)}, u32[]{:S(2)}, u32[]{:S(2)}) async-start(bf16[4,2,16,2048]{3,2,1,0:T(8,128)(2,1)} %bitcast.19), calls=%async_computation.3 | async-start | bytes 1048576 | tf_op jit(solution)/shard_map/all_to_all | solution.py:150
  40.0 2.0 %convolution_convert_fusion = bf16[128,2048]{1,0:T(8,128)(2,1)} fusion(bf16[1,176,2048]{2,1,0:T(8,128)(2,1)S(1)} %copy-done.4, f32[128,176]{0,1:T(8,128)} %fusion.39, f32[128,176]{0,1:T(8,128)S(1)} %fusion.43), kind=kOutput, calls=%fused_computation.33 | convolution fusion | flops 92672000 | bytes 1425408 | tf_op jit(solution)/shard_map/dot_general | solution.py:39
  42.0 0.4 reduce_max.40
  42.6 1.2 %fusion.33 = (f32[8]{0:T(128)S(1)}, f32[8]{0:T(128)S(1)}, f32[8]{0:T(128)S(1)}, f32[8]{0:T(128)S(1)}) fusion(bf16[1,8,37984]{2,1,0:T(8,128)(2,1)S(1)} %collective-permute-done, bf16[1,8,37984]{2,1,0:T(8,128)(2,1)S(1)} %copy-done.1, f32[8]{0:T(128)S(1)} %reduce_max.45, s32[8]{0:T(128)S(1)} %bitcast.137, s32[37984]{0:T(1024)S(1)} %iota_add_fusion, ...), kind=kLoop, calls=%fused_computation.56 | loop fusion | flops 3646432 | bytes 1367648 | tf_op jit(solution)/shard_map/reduce_sum | solution.py:87
  44.6 7.3 %all-reduce.6 = (f32[32]{0:T(128)S(1)}, f32[32]{0:T(128)S(1)}, f32[32]{0:T(128)S(1)}, f32[32]{0:T(128)S(1)}, f32[32]{0:T(128)S(1)}, /*index=5*/f32[32]{0:T(128)S(1)}) all-reduce(f32[32]{0:T(128)S(1)} %convert_dynamic-update-slice_fusion.1, f32[32]{0:T(128)S(1)} %dynamic-update-slice.1, ...), channel_id=2, replica_groups=mesh['peer'=8,'grp'=4] {'grp'}, use_global_device_ids=true, to_apply=%add | all-reduce | flops 192 | bytes 1536
  52.7 0.5 subtract_bitcast_fusion
  53.2 3.7 %all-to-all-start.1 = ((bf16[4,2,16,2048]{3,2,1,0:T(8,128)(2,1)}), bf16[4,2,16,2048]{3,2,1,0:T(8,128)(2,1)S(1)}, u32[]{:S(2)}, u32[]{:S(2)}) async-start(bf16[4,2,16,2048]{3,2,1,0:T(8,128)(2,1)} %bitcast.128), calls=%async_computation.1 | async-start | bytes 1048576 | tf_op jit(solution)/shard_map/all_to_all | solution.py:149
  56.9 1.4 %fusion.29 = bf16[1,8,37984]{2,1,0:T(8,128)(2,1)} fusion(bf16[1,8,37984]{2,1,0:T(8,128)(2,1)S(1)} %copy-done.1, bf16[1,8,37984]{2,1,0:T(8,128)(2,1)S(1)} %collective-permute-done, f32[8]{0:T(128)S(1)} %get-tuple-element.380, s32[37984]{0:T(1024)S(1)} %iota_add_fusion, f32[8]{0:T(128)S(1)} %get-tuple-element.379, s32[8]{0:T(128)S(1)} %bitcast.138), kind=kLoop, calls=%fused_computation.52 | loop fusion | flops 3038720 | bytes 1975264 | tf_op jit(solution)/shard_map/convert_element_type | solution.py:99
  58.4 3.6 %gather_fusion.2 = f32[512,2048]{1,0:T(8,128)} fusion(f32[32,2048]{1,0:T(8,128)S(1)} %bitcast.125, s32[1024]{0:T(1024)S(1)} %pad_clamp_fusion), kind=kCustom, calls=%fused_computation.1.clone | custom fusion | bytes 8390656 | tf_op jit(solution)/shard_map/jit(_take)/gather | solution.py:169
  62.0 5.2 %reshape.355 = f32[128,4,2048]{2,1,0:T(4,128)} reshape(f32[512,2048]{1,0:T(8,128)} %gather_fusion.2) | data formatting | bytes 8388608 | tf_op jit(solution)/shard_map/jit(_take)/gather | solution.py:169
  67.3 3.6 %gather_fusion.1 = f32[512,2048]{1,0:T(8,128)} fusion(f32[32,2048]{1,0:T(8,128)S(1)} %bitcast.124, s32[1024]{0:T(1024)S(1)} %pad_clamp_fusion), kind=kCustom, calls=%fused_computation.clone | custom fusion | bytes 8390656 | tf_op jit(solution)/shard_map/jit(_take)/gather | solution.py:164
  70.9 5.3 %reshape.351 = f32[128,4,2048]{2,1,0:T(4,128)} reshape(f32[512,2048]{1,0:T(8,128)} %gather_fusion.1) | data formatting | bytes 8388608 | tf_op jit(solution)/shard_map/jit(_take)/gather | solution.py:164
  76.1 11.4 %multiply_reduce_fusion = (f32[128,4]{1,0:T(8,128)S(1)}, bf16[128,2048]{1,0:T(8,128)(2,1)}, bf16[128,2048]{1,0:T(8,128)(2,1)}) fusion(f32[128,4,2048]{2,1,0:T(4,128)} %reshape.351, f32[128,2048]{1,0:T(8,128)S(1)} %copy-done.2, pred[128,4]{1,0:T(8,128)(4,1)S(1)} %copy.46, pred[128,4]{1,0:T(8,128)(4,1)S(1)} %copy.41, f32[128,4]{1,0:T(8,128)S(1)} %copy-done.7, ...), kind=kLoop, calls=%fused_computation.29 | loop fusion | flops 8912384 | bytes 10490880 | tf_op jit(solution)/shard_map/reduce_sum | solution.py:173
  87.5 0.7 copy.50
  (83 shorter events, 4.2 us)
Async XLA Ops:
  0.6 23.7 %copy-start = (bf16[1,2048,176]{1,2,0:T(8,128)(2,1)S(1)}, bf16[1,2048,176]{1,2,0:T(8,128)(2,1)}, u32[]{:S(2)}) copy-start(bf16[1,2048,176]{1,2,0:T(8,128)(2,1)} %param.18) | copy-start | bytes 2162692
  0.6 41.4 %collective-permute-start = (bf16[1,8,37984]{2,1,0:T(8,128)(2,1)}, bf16[1,8,37984]{2,1,0:T(8,128)(2,1)S(1)}, u32[]{:S(2)}, u32[]{:S(2)}) collective-permute-start(bf16[1,8,37984]{2,1,0:T(8,128)(2,1)} %param.22), channel_id=1, source_target_pairs={{0,4},{4,8},{8,12},{12,16},{16,20},{20,24},{24,28},{28,0},{1,5},{5... | collective-permute-start | bytes 1823240 | tf_op jit(solution)/shard_map/ppermute | solution.py:23
  4.8 5.6 %copy-start.8 = (s32[128,4]{0,1:T(4,128)S(1)}, s32[128,4]{0,1:T(4,128)}, u32[]{:S(2)}) copy-start(s32[128,4]{0,1:T(4,128)} %param.16) | copy-start | bytes 6148
  7.0 12.3 %all-to-all-start = ((bf16[4,2,16,2048]{3,2,1,0:T(8,128)(2,1)}), bf16[4,2,16,2048]{3,2,1,0:T(8,128)(2,1)S(1)}, u32[]{:S(2)}, u32[]{:S(2)}) async-start(bf16[4,2,16,2048]{3,2,1,0:T(8,128)(2,1)} %broadcast_in_dim.63), calls=%async_computation | async-start | bytes 1048576 | tf_op jit(solution)/shard_map/all_to_all | solution.py:140
  10.7 3.9 %copy-start.1 = (bf16[1,8,37984]{2,1,0:T(8,128)(2,1)S(1)}, bf16[1,8,37984]{2,1,0:T(8,128)(2,1)}, u32[]{:S(2)}) copy-start(bf16[1,8,37984]{2,1,0:T(8,128)(2,1)} %param.21) | copy-start | bytes 1823236
  10.7 4.3 %copy-start.11 = (u32[32]{0:T(128)S(1)}, u32[32]{0:T(128)}, u32[]{:S(2)}) copy-start(u32[32]{0:T(128)} %constant.107) | copy-start | bytes 388
  10.7 5.7 %copy-start.9 = (f32[128,4]{0,1:T(4,128)S(1)}, f32[128,4]{0,1:T(4,128)}, u32[]{:S(2)}) copy-start(f32[128,4]{0,1:T(4,128)} %param.17) | copy-start | bytes 6148
  14.2 3.3 %copy-start.5 = (bf16[128,2048]{1,0:T(8,128)(2,1)S(1)}, bf16[128,2048]{1,0:T(8,128)(2,1)}, u32[]{:S(2)}) copy-start(bf16[128,2048]{1,0:T(8,128)(2,1)} %param.15) | copy-start | bytes 1572868
  20.1 4.7 %copy-start.3 = (bf16[1,2048,176]{1,2,0:T(8,128)(2,1)S(1)}, bf16[1,2048,176]{1,2,0:T(8,128)(2,1)}, u32[]{:S(2)}) copy-start(bf16[1,2048,176]{1,2,0:T(8,128)(2,1)} %param.19) | copy-start | bytes 2162692
  20.1 13.1 %all-to-all-start.2 = ((bf16[4,2,16,2048]{3,2,1,0:T(8,128)(2,1)}), bf16[4,2,16,2048]{3,2,1,0:T(8,128)(2,1)}, u32[]{:S(2)}, u32[]{:S(2)}) async-start(bf16[4,2,16,2048]{3,2,1,0:T(8,128)(2,1)} %broadcast_in_dim.67), calls=%async_computation.2 | async-start | bytes 1048576 | tf_op jit(solution)/shard_map/all_to_all | solution.py:141
  25.8 9.1 %copy-start.6 = (f32[128,176]{0,1:T(8,128)S(1)}, f32[128,176]{0,1:T(8,128)}, u32[]{:S(2)}) copy-start(f32[128,176]{0,1:T(8,128)} %fusion.39) | copy-start | bytes 270340
  36.4 3.6 %copy-start.4 = (bf16[1,176,2048]{2,1,0:T(8,128)(2,1)S(1)}, bf16[1,176,2048]{2,1,0:T(8,128)(2,1)}, u32[]{:S(2)}) copy-start(bf16[1,176,2048]{2,1,0:T(8,128)(2,1)} %param.20) | copy-start | bytes 2162692
  36.4 16.9 %all-to-all-start.3 = ((bf16[4,2,16,2048]{3,2,1,0:T(8,128)(2,1)}), bf16[4,2,16,2048]{3,2,1,0:T(8,128)(2,1)S(1)}, u32[]{:S(2)}, u32[]{:S(2)}) async-start(bf16[4,2,16,2048]{3,2,1,0:T(8,128)(2,1)} %bitcast.19), calls=%async_computation.3 | async-start | bytes 1048576 | tf_op jit(solution)/shard_map/all_to_all | solution.py:150
  40.0 2.6 %copy-start.10 = (s32[1,8]{1,0:T(1,128)S(1)}, s32[1,8]{1,0:T(1,128)}, u32[]{:S(2)}) copy-start(s32[1,8]{1,0:T(1,128)} %param.23) | copy-start | bytes 100
  53.2 14.0 %all-to-all-start.1 = ((bf16[4,2,16,2048]{3,2,1,0:T(8,128)(2,1)}), bf16[4,2,16,2048]{3,2,1,0:T(8,128)(2,1)S(1)}, u32[]{:S(2)}, u32[]{:S(2)}) async-start(bf16[4,2,16,2048]{3,2,1,0:T(8,128)(2,1)} %bitcast.128), calls=%async_computation.1 | async-start | bytes 1048576 | tf_op jit(solution)/shard_map/all_to_all | solution.py:149
  70.9 5.3 %copy-start.2 = (f32[128,2048]{1,0:T(8,128)S(1)}, f32[128,2048]{1,0:T(8,128)}, u32[]{:S(2)}) copy-start(f32[128,2048]{1,0:T(8,128)} %convert_element_type.89) | copy-start | bytes 3145732
  70.9 5.3 %copy-start.7 = (f32[128,4]{1,0:T(8,128)S(1)}, f32[128,4]{1,0:T(8,128)}, u32[]{:S(2)}) copy-start(f32[128,4]{1,0:T(8,128)} %copy.40) | copy-start | bytes 6148
where the time goes:
time: 88.8 us; the launch traced here: 88.1 us
  local copies, waits for them, and re-layouts  27.1 us (31%)
  other arithmetic  18.1 us (20%)
  starting transfers between devices  18 us (20%)
  matrix products  8.18 us (9%)
  waiting for transfers between devices  7.67 us (9%)
  blocking collectives  7.33 us (8%)
  between operations  1.6 us (2%)
    reduce_sum x1, other arithmetic, body(): jnp.sum(cotangent.astype(jnp.float32)[:, None, :] * out_rows, axis=2)  11.4 us
    gather x2, local copies, waits for them, and re-layouts, body(): jnp.take(expert_out.reshape(-1, model_width), flat_index, axis=0)  8.83 us
    gather x2, local copies, waits for them, and re-layouts, body(): jnp.take(expert_grad.reshape(-1, model_width), flat_index, axis=0)  8.79 us
    all_to_all x1, waiting for transfers between devices, body(): lax.all_to_all(send_scaled, 'grp', split_axis=0, concat_axis=0, tiled=True)  7.41 us
    unnamed x1, blocking collectives  7.33 us
    all_to_all x1, starting transfers between devices, body(): lax.all_to_all(send_scaled, 'grp', split_axis=0, concat_axis=0, tiled=True)  4.26 us
    gather x5, local copies, waits for them, and re-layouts, body(): slot_index = jnp.take_along_axis(position, safe_ids, axis=1)  3.81 us
    all_to_all x1, starting transfers between devices, body(): lax.all_to_all(piece_out, 'grp', split_axis=0, concat_axis=0, tiled=True)  3.65 us
  transfers between devices with their start and end apart: 5, of which 2 were waited for; matrix products, arithmetic and copies ran while one was open for 37% of the time, Pallas kernels for 0%

commit v1 on v0

--- a/solution.py
+++ b/solution.py
@@ -5,6 +5,22 @@
 
 PIECES = 4
 CAP = 32
+
+
+def exchange_in_pairs(x, axis, split, join):
+    ways, here = (lax.axis_size(axis), lax.axis_index(axis))
+    width = x.shape[split] // ways
+    shape = list(x.shape)
+    shape[split] = width
+    height = shape[join]
+    shape[join] = height * ways
+    full = jnp.zeros(shape, x.dtype)
+    for mask in range(ways):
+        part = lax.dynamic_slice_in_dim(x, (here ^ mask) * width, width, axis=split)
+        if mask:
+            part = lax.ppermute(part, axis, [(d, d ^ mask) for d in range(ways)])
+        full = lax.dynamic_update_slice_in_dim(full, part, (here ^ mask) * height, axis=join)
+    return full
 
 
 def joined(value, axis, combine):
@@ -138,7 +154,7 @@
         group_size, 2, half_cap, model_width
     )
     recv_rows = lax.all_to_all(send_rows, "grp", split_axis=0, concat_axis=0, tiled=True)
-    recv_scaled = lax.all_to_all(send_scaled, "grp", split_axis=0, concat_axis=0, tiled=True)
+    recv_scaled = exchange_in_pairs(send_scaled, "grp", 0, 0)
     item_count = recv_rows.shape[1]
     flat_rows = recv_rows.reshape(-1, model_width)
     flat_scaled = recv_scaled.reshape(-1, model_width)

time: 88.8 us -> 84.9 us (0.956)
  waiting for transfers between devices: 7.67 us -> 0.02 us
  local copies, waits for them, and re-layouts: 27.1 us -> 33.1 us
  starting transfers between devices: 18 us -> 15.6 us
    all_to_all x1 -> x0, waiting for transfers between devices: 7.41 us -> none  [body(): lax.all_to_all(send_scaled, 'grp', split_axis=0, concat_axis=0, tiled=True)]
    dynamic_update_slice x0 -> x4, local copies, waits for them, and re-layouts: none -> 5.37 us  [exchange_in_pairs(): lax.dynamic_update_slice_in_dim(full, part, (here ^ mask) * height, axis=...]
    all_to_all x1 -> x0, starting transfers between devices: 4.26 us -> none  [body(): lax.all_to_all(send_scaled, 'grp', split_axis=0, concat_axis=0, tiled=True)]
    ppermute x0 -> x3, starting transfers between devices: none -> 3.15 us  [exchange_in_pairs(): part = lax.ppermute(part, axis, [(d, d ^ mask) for d in range(ways)])]
    ppermute x1, starting transfers between devices: 3.05 us -> 1.77 us  [from_behind(): return lax.ppermute(value, axis, pairs)]
    dot_general x1, matrix products: 1.24 us -> 0.19 us  [body(): jnp.einsum('ect,td->ecd', select_bf, tokens, preferred_element_type=jnp.f...]
    dot_general x1, matrix products: 0.22 us -> 1.27 us  [body(): jnp.einsum('ect,td->ecd', select_bf, cotangent, preferred_element_type=jn...]
    unnamed x37 -> x41, local copies, waits for them, and re-layouts: 2.89 us -> 3.52 us
  transfers between devices with their start and end apart: 5 -> 7, of which waited for: 2 -> 0; matrix products, arithmetic and copies ran while one was open for 37% -> 42% of each run, Pallas kernels for 0% -> 0%
where the time goes in v1:
time: 84.9 us; the launch traced here: 84.2 us
  local copies, waits for them, and re-layouts  33.1 us (39%)
  other arithmetic  18.2 us (21%)
  starting transfers between devices  15.6 us (18%)
  matrix products  8.2 us (10%)
  blocking collectives  7.33 us (9%)
  between operations  1.61 us (2%)
    reduce_sum x1, other arithmetic, body(): jnp.sum(cotangent.astype(jnp.float32)[:, None, :] * out_rows, axis=2)  11.4 us
    gather x2, local copies, waits for them, and re-layouts, body(): jnp.take(expert_out.reshape(-1, model_width), flat_index, axis=0)  8.83 us
    gather x2, local copies, waits for them, and re-layouts, body(): jnp.take(expert_grad.reshape(-1, model_width), flat_index, axis=0)  8.79 us
    unnamed x1, blocking collectives  7.33 us
    dynamic_update_slice x4, local copies, waits for them, and re-layouts, exchange_in_pairs(): lax.dynamic_update_slice_in_dim(full, part, (here ^ mask) * height, axis=...  5.37 us
    gather x5, local copies, waits for them, and re-layouts, body(): slot_index = jnp.take_along_axis(position, safe_ids, axis=1)  3.81 us
    all_to_all x1, starting transfers between devices, body(): lax.all_to_all(piece_out, 'grp', split_axis=0, concat_axis=0, tiled=True)  3.65 us
    all_to_all x1, starting transfers between devices, body(): lax.all_to_all(piece_grad, 'grp', split_axis=0, concat_axis=0, tiled=True)  3.6 us
  transfers between devices with their start and end apart: 7, of which 0 were waited for; matrix products, arithmetic and copies ran while one was open for 42% of the time, Pallas kernels for 0%

profile of v1, /device:TPU:0, one launch (start us, length us, event | category | flops | bytes accessed | tf_op | source)
XLA Modules:
  0.0 84.2 jit_solution(3172505145111833586)
XLA Ops:
  0.7 0.8 select_reduce_fusion
  2.0 1.3 %fusion.17 = bf16[32,2048]{1,0:T(8,128)(2,1)S(1)} fusion(bf16[128,2048]{1,0:T(8,128)(2,1)} %param.15, f32[32]{0:T(128)S(1)} %convolution_bitcast_fusion, s32[128]{0:T(128)S(1)} %sub.111, pred[128]{0:T(512)(128)(4,1)S(1)} %broadcast_compare_fusion.2), kind=kOutput, calls=%fused_computation.35 | convolution fusion | flops 16916480 | bytes 656128 | tf_op jit(solution)/shard_map/ect,td->ecd/dot_general | solution.py:150
  3.3 0.6 collective-permute-start
  3.9 2.6 %collective-permute-start.1 = (bf16[1,2,16,2048]{3,2,1,0:T(8,128)(2,1)S(1)}, bf16[1,2,16,2048]{3,2,1,0:T(8,128)(2,1)}, u32[]{:S(2)}, u32[]{:S(2)}) collective-permute-start(bf16[1,2,16,2048]{3,2,1,0:T(8,128)(2,1)S(1)} %bitcast.131), channel_id=1, source_target_pairs={{0,2},{1,3},{2,0},{3,1},{4,6},{5,7},{6,4},{7,5},{8,10},{9,11},{10,... | collective-permute-start | bytes 393224 | tf_op jit(solution)/shard_map/ppermute | solution.py:21
  6.5 1.8 %collective-permute-start.3 = (bf16[1,8,37984]{2,1,0:T(8,128)(2,1)}, bf16[1,8,37984]{2,1,0:T(8,128)(2,1)S(1)}, u32[]{:S(2)}, u32[]{:S(2)}) collective-permute-start(bf16[1,8,37984]{2,1,0:T(8,128)(2,1)} %param.22), channel_id=1, source_target_pairs={{0,4},{4,8},{8,12},{12,16},{16,20},{20,24},{24,28},{28,0},{1,5},{5... | collective-permute-start | bytes 1823240 | tf_op jit(solution)/shard_map/ppermute | solution.py:39
  8.4 0.9 %broadcast_in_dim.64 = bf16[4,2,16,2048]{3,2,1,0:T(8,128)(2,1)} broadcast(bf16[2,16,2048]{2,1,0:T(8,128)(2,1)S(1)} %bitcast.129), dimensions={1,2,3} | broadcast | bytes 655360 | tf_op jit(solution)/shard_map/broadcast_in_dim | solution.py:152
  9.3 3.5 %all-to-all-start = ((bf16[4,2,16,2048]{3,2,1,0:T(8,128)(2,1)}), bf16[4,2,16,2048]{3,2,1,0:T(8,128)(2,1)S(1)}, u32[]{:S(2)}, u32[]{:S(2)}) async-start(bf16[4,2,16,2048]{3,2,1,0:T(8,128)(2,1)} %broadcast_in_dim.64), calls=%async_computation | async-start | bytes 1048576 | tf_op jit(solution)/shard_map/all_to_all | solution.py:156
  13.1 3.4 %gather_fusion = s32[512]{0:T(512)S(1)} fusion(s32[128,1]{1,0:T(8,128)S(1)} %get-tuple-element.386, s32[512]{0:T(512)S(1)} %reshape.293), kind=kCustom, calls=%fused_computation.2 | custom fusion | bytes 8192 | tf_op jit(solution)/shard_map/jit(take_along_axis)/gather | solution.py:176
  17.2 0.6 dynamic-slice.4
  18.4 0.8 %broadcast_in_dim.67 = bf16[4,2,16,2048]{3,2,1,0:T(8,128)(2,1)} broadcast(bf16[]{:T(256)} %constant.86.clone.1), dimensions={} | broadcast | bytes 524290 | tf_op jit(solution)/shard_map/broadcast_in_dim | solution.py:17
  19.3 0.7 constant_dynamic-update-slice_fusion.3
  20.0 1.2 %convert_element_type.89 = f32[128,2048]{1,0:T(8,128)} convert(bf16[128,2048]{1,0:T(8,128)(2,1)S(1)} %copy-done.5) | non-fusion elementwise | flops 262144 | bytes 1572864 | tf_op jit(solution)/shard_map/convert_element_type | solution.py:189
  21.2 0.7 copy.40
  22.5 1.6 %constant_dynamic-update-slice_fusion.2 = bf16[4,2,16,2048]{3,2,1,0:T(8,128)(2,1)} fusion(bf16[4,2,16,2048]{3,2,1,0:T(8,128)(2,1)} %constant_dynamic-update-slice_fusion.3, bf16[1,2,16,2048]{3,2,1,0:T(8,128)(2,1)} %collective-permute-done, s32[]{:T(128)S(6)} %select_n.66), kind=kLoop, calls=%fused_computation.97 | loop fusion | bytes 262148 | tf_op jit(solution)/shard_map/dynamic_update_slice | solution.py:22
  24.0 1.6 %constant_dynamic-update-slice_fusion.1 = bf16[4,2,16,2048]{3,2,1,0:T(8,128)(2,1)} fusion(bf16[4,2,16,2048]{3,2,1,0:T(8,128)(2,1)} %constant_dynamic-update-slice_fusion.2, bf16[1,2,16,2048]{3,2,1,0:T(8,128)(2,1)} %collective-permute-done.1, s32[]{:T(128)S(6)} %select_n.67), kind=kLoop, calls=%fused_computation.96 | loop fusion | bytes 262148 | tf_op jit(solution)/shard_map/dynamic_update_slice | solution.py:22
  25.6 1.6 %constant_dynamic-update-slice_fusion = bf16[4,2,16,2048]{3,2,1,0:T(8,128)(2,1)} fusion(bf16[4,2,16,2048]{3,2,1,0:T(8,128)(2,1)} %constant_dynamic-update-slice_fusion.1, bf16[1,2,16,2048]{3,2,1,0:T(8,128)(2,1)} %collective-permute-done.2, s32[]{:T(128)S(6)} %select_n.68), kind=kLoop, calls=%fused_computation.95 | loop fusion | bytes 262148 | tf_op jit(solution)/shard_map/dynamic_update_slice | solution.py:22
  27.2 2.3 %fusion.35 = f32[128,176]{0,1:T(8,128)} fusion(bf16[128,2048]{1,0:T(8,128)(2,1)} %bitcast.18, bf16[1,176,2048]{2,1,0:T(8,128)(2,1)} %param.20), kind=kOutput, calls=%fused_computation.61 | convolution fusion | flops 92274688 | bytes 1335296 | tf_op jit(solution)/shard_map/dot_general | solution.py:61
  30.3 0.6 copy-done.7
  31.3 1.1 %fusion.16 = bf16[128,2048]{1,0:T(8,128)(2,1)} fusion(f32[128,2048]{1,0:T(8,128)S(1)} %fusion.41, bf16[1,2048,176]{1,2,0:T(8,128)(2,1)S(1)} %copy-done.3, f32[128,176]{0,1:T(8,128)S(1)} %copy-done.6, f32[128,176]{0,1:T(8,128)S(1)} %fusion.43), kind=kOutput, calls=%fused_computation.32 | convolution fusion | flops 92934144 | bytes 2473984 | tf_op jit(solution)/shard_map/dot_general | solution.py:70
  32.5 3.6 %all-to-all-start.2 = ((bf16[4,2,16,2048]{3,2,1,0:T(8,128)(2,1)}), bf16[4,2,16,2048]{3,2,1,0:T(8,128)(2,1)S(1)}, u32[]{:S(2)}, u32[]{:S(2)}) async-start(bf16[4,2,16,2048]{3,2,1,0:T(8,128)(2,1)} %bitcast.19), calls=%async_computation.2 | async-start | bytes 1048576 | tf_op jit(solution)/shard_map/all_to_all | solution.py:166
  36.1 2.0 %convolution_convert_fusion = bf16[128,2048]{1,0:T(8,128)(2,1)} fusion(bf16[1,176,2048]{2,1,0:T(8,128)(2,1)S(1)} %copy-done.4, f32[128,176]{0,1:T(8,128)} %copy-done.7, f32[128,176]{0,1:T(8,128)S(1)} %fusion.43), kind=kOutput, calls=%fused_computation.33 | convolution fusion | flops 92672000 | bytes 1425408 | tf_op jit(solution)/shard_map/dot_general | solution.py:55
  38.7 1.2 %fusion.33 = (f32[8]{0:T(128)S(1)}, f32[8]{0:T(128)S(1)}, f32[8]{0:T(128)S(1)}, f32[8]{0:T(128)S(1)}) fusion(bf16[1,8,37984]{2,1,0:T(8,128)(2,1)S(1)} %collective-permute-done.3, bf16[1,8,37984]{2,1,0:T(8,128)(2,1)S(1)} %copy-done.1, f32[8]{0:T(128)S(1)} %reduce_max.45, s32[8]{0:T(128)S(1)} %bitcast.140, s32[37984]{0:T(1024)S(1)} %iota_add_fusion, ...), kind=kLoop, calls=%fused_computation.56 | loop fusion | flops 3646432 | bytes 1367648 | tf_op jit(solution)/shard_map/reduce_sum | solution.py:103
  40.7 7.3 %all-reduce.6 = (f32[32]{0:T(128)S(1)}, f32[32]{0:T(128)S(1)}, f32[32]{0:T(128)S(1)}, f32[32]{0:T(128)S(1)}, f32[32]{0:T(128)S(1)}, /*index=5*/f32[32]{0:T(128)S(1)}) all-reduce(f32[32]{0:T(128)S(1)} %convert_dynamic-update-slice_fusion.1, f32[32]{0:T(128)S(1)} %dynamic-update-slice.1, ...), channel_id=2, replica_groups=mesh['peer'=8,'grp'=4] {'grp'}, use_global_device_ids=true, to_apply=%add | all-reduce | flops 192 | bytes 1536
  48.8 0.5 subtract_bitcast_fusion
  49.3 3.7 %all-to-all-start.1 = ((bf16[4,2,16,2048]{3,2,1,0:T(8,128)(2,1)}), bf16[4,2,16,2048]{3,2,1,0:T(8,128)(2,1)S(1)}, u32[]{:S(2)}, u32[]{:S(2)}) async-start(bf16[4,2,16,2048]{3,2,1,0:T(8,128)(2,1)} %bitcast.128), calls=%async_computation.1 | async-start | bytes 1048576 | tf_op jit(solution)/shard_map/all_to_all | solution.py:165
  53.0 1.4 %fusion.29 = bf16[1,8,37984]{2,1,0:T(8,128)(2,1)} fusion(bf16[1,8,37984]{2,1,0:T(8,128)(2,1)S(1)} %copy-done.1, bf16[1,8,37984]{2,1,0:T(8,128)(2,1)S(1)} %collective-permute-done.3, f32[8]{0:T(128)S(1)} %get-tuple-element.380, s32[37984]{0:T(1024)S(1)} %iota_add_fusion, f32[8]{0:T(128)S(1)} %get-tuple-element.379, s32[8]{0:T(128)S(1)} %bitcast.141), kind=kLoop, calls=%fused_computation.52 | loop fusion | flops 3038720 | bytes 1975264 | tf_op jit(solution)/shard_map/convert_element_type | solution.py:115
  54.5 3.6 %gather_fusion.2 = f32[512,2048]{1,0:T(8,128)} fusion(f32[32,2048]{1,0:T(8,128)S(1)} %bitcast.125, s32[1024]{0:T(1024)S(1)} %pad_clamp_fusion), kind=kCustom, calls=%fused_computation.1.clone | custom fusion | bytes 8390656 | tf_op jit(solution)/shard_map/jit(_take)/gather | solution.py:185
  58.1 5.2 %reshape.363 = f32[128,4,2048]{2,1,0:T(4,128)} reshape(f32[512,2048]{1,0:T(8,128)} %gather_fusion.2) | data formatting | bytes 8388608 | tf_op jit(solution)/shard_map/jit(_take)/gather | solution.py:185
  63.4 3.6 %gather_fusion.1 = f32[512,2048]{1,0:T(8,128)} fusion(f32[32,2048]{1,0:T(8,128)S(1)} %bitcast.124, s32[1024]{0:T(1024)S(1)} %pad_clamp_fusion), kind=kCustom, calls=%fused_computation.clone | custom fusion | bytes 8390656 | tf_op jit(solution)/shard_map/jit(_take)/gather | solution.py:180
  67.0 5.3 %reshape.359 = f32[128,4,2048]{2,1,0:T(4,128)} reshape(f32[512,2048]{1,0:T(8,128)} %gather_fusion.1) | data formatting | bytes 8388608 | tf_op jit(solution)/shard_map/jit(_take)/gather | solution.py:180
  72.2 11.4 %multiply_reduce_fusion = (f32[128,4]{1,0:T(8,128)S(1)}, bf16[128,2048]{1,0:T(8,128)(2,1)}, bf16[128,2048]{1,0:T(8,128)(2,1)}) fusion(f32[128,4,2048]{2,1,0:T(4,128)} %reshape.359, f32[128,2048]{1,0:T(8,128)S(1)} %copy-done.2, pred[128,4]{1,0:T(8,128)(4,1)S(1)} %copy.46, pred[128,4]{1,0:T(8,128)(4,1)S(1)} %copy.41, f32[128,4]{1,0:T(8,128)S(1)} %copy-done.9, ...), kind=kLoop, calls=%fused_computation.29 | loop fusion | flops 8912384 | bytes 10490880 | tf_op jit(solution)/shard_map/reduce_sum | solution.py:189
  83.6 0.7 copy.50
  (95 shorter events, 6.0 us)
Async XLA Ops:
  0.6 28.9 %copy-start = (bf16[1,2048,176]{1,2,0:T(8,128)(2,1)S(1)}, bf16[1,2048,176]{1,2,0:T(8,128)(2,1)}, u32[]{:S(2)}) copy-start(bf16[1,2048,176]{1,2,0:T(8,128)(2,1)} %param.18) | copy-start | bytes 2162692
  0.6 7.6 %copy-start.8 = (bf16[128,2048]{1,0:T(8,128)(2,1)S(1)}, bf16[128,2048]{1,0:T(8,128)(2,1)}, u32[]{:S(2)}) copy-start(bf16[128,2048]{1,0:T(8,128)(2,1)} %param.14) | copy-start | bytes 1572868
  3.3 9.5 %copy-start.10 = (s32[128,4]{0,1:T(4,128)S(1)}, s32[128,4]{0,1:T(4,128)}, u32[]{:S(2)}) copy-start(s32[128,4]{0,1:T(4,128)} %param.16) | copy-start | bytes 6148
  3.3 19.1 %collective-permute-start = (bf16[1,2,16,2048]{3,2,1,0:T(8,128)(2,1)S(1)}, bf16[1,2,16,2048]{3,2,1,0:T(8,128)(2,1)}, u32[]{:S(2)}, u32[]{:S(2)}) collective-permute-start(bf16[1,2,16,2048]{3,2,1,0:T(8,128)(2,1)S(1)} %bitcast.130), channel_id=1, source_target_pairs={{0,1},{1,0},{2,3},{3,2},{4,5},{5,4},{6,7},{7,6},{8,9},{9,8},{10,11... | collective-permute-start | bytes 393224 | tf_op jit(solution)/shard_map/ppermute | solution.py:21
  3.9 20.2 %collective-permute-start.1 = (bf16[1,2,16,2048]{3,2,1,0:T(8,128)(2,1)S(1)}, bf16[1,2,16,2048]{3,2,1,0:T(8,128)(2,1)}, u32[]{:S(2)}, u32[]{:S(2)}) collective-permute-start(bf16[1,2,16,2048]{3,2,1,0:T(8,128)(2,1)S(1)} %bitcast.131), channel_id=1, source_target_pairs={{0,2},{1,3},{2,0},{3,1},{4,6},{5,7},{6,4},{7,5},{8,10},{9,11},{10,... | collective-permute-start | bytes 393224 | tf_op jit(solution)/shard_map/ppermute | solution.py:21
  6.4 19.2 %collective-permute-start.2 = (bf16[1,2,16,2048]{3,2,1,0:T(8,128)(2,1)S(1)}, bf16[1,2,16,2048]{3,2,1,0:T(8,128)(2,1)}, u32[]{:S(2)}, u32[]{:S(2)}) collective-permute-start(bf16[1,2,16,2048]{3,2,1,0:T(8,128)(2,1)S(1)} %bitcast.132), channel_id=1, source_target_pairs={{0,3},{1,2},{2,1},{3,0},{4,7},{5,6},{6,5},{7,4},{8,11},{9,10},{10,... | collective-permute-start | bytes 393224 | tf_op jit(solution)/shard_map/ppermute | solution.py:21
  6.5 31.7 %collective-permute-start.3 = (bf16[1,8,37984]{2,1,0:T(8,128)(2,1)}, bf16[1,8,37984]{2,1,0:T(8,128)(2,1)S(1)}, u32[]{:S(2)}, u32[]{:S(2)}) collective-permute-start(bf16[1,8,37984]{2,1,0:T(8,128)(2,1)} %param.22), channel_id=1, source_target_pairs={{0,4},{4,8},{8,12},{12,16},{16,20},{20,24},{24,28},{28,0},{1,5},{5... | collective-permute-start | bytes 1823240 | tf_op jit(solution)/shard_map/ppermute | solution.py:39
  9.3 20.2 %all-to-all-start = ((bf16[4,2,16,2048]{3,2,1,0:T(8,128)(2,1)}), bf16[4,2,16,2048]{3,2,1,0:T(8,128)(2,1)S(1)}, u32[]{:S(2)}, u32[]{:S(2)}) async-start(bf16[4,2,16,2048]{3,2,1,0:T(8,128)(2,1)} %broadcast_in_dim.64), calls=%async_computation | async-start | bytes 1048576 | tf_op jit(solution)/shard_map/all_to_all | solution.py:156
  13.1 3.7 %copy-start.1 = (bf16[1,8,37984]{2,1,0:T(8,128)(2,1)S(1)}, bf16[1,8,37984]{2,1,0:T(8,128)(2,1)}, u32[]{:S(2)}) copy-start(bf16[1,8,37984]{2,1,0:T(8,128)(2,1)} %param.21) | copy-start | bytes 1823236
  13.1 4.1 %copy-start.13 = (u32[32]{0:T(128)S(1)}, u32[32]{0:T(128)}, u32[]{:S(2)}) copy-start(u32[32]{0:T(128)} %constant.115) | copy-start | bytes 388
  16.5 3.5 %copy-start.5 = (bf16[128,2048]{1,0:T(8,128)(2,1)S(1)}, bf16[128,2048]{1,0:T(8,128)(2,1)}, u32[]{:S(2)}) copy-start(bf16[128,2048]{1,0:T(8,128)(2,1)} %param.15) | copy-start | bytes 1572868
  17.2 4.0 %copy-start.11 = (f32[128,4]{0,1:T(4,128)S(1)}, f32[128,4]{0,1:T(4,128)}, u32[]{:S(2)}) copy-start(f32[128,4]{0,1:T(4,128)} %param.17) | copy-start | bytes 6148
  27.2 2.7 %copy-start.3 = (bf16[1,2048,176]{1,2,0:T(8,128)(2,1)S(1)}, bf16[1,2048,176]{1,2,0:T(8,128)(2,1)}, u32[]{:S(2)}) copy-start(bf16[1,2048,176]{1,2,0:T(8,128)(2,1)} %param.19) | copy-start | bytes 2162692
  29.5 1.4 %copy-start.6 = (f32[128,176]{0,1:T(8,128)S(1)}, f32[128,176]{0,1:T(8,128)}, u32[]{:S(2)}) copy-start(f32[128,176]{0,1:T(8,128)} %fusion.35) | copy-start | bytes 270340
  30.3 0.6 copy-start.7
  32.5 3.6 %copy-start.4 = (bf16[1,176,2048]{2,1,0:T(8,128)(2,1)S(1)}, bf16[1,176,2048]{2,1,0:T(8,128)(2,1)}, u32[]{:S(2)}) copy-start(bf16[1,176,2048]{2,1,0:T(8,128)(2,1)} %param.20) | copy-start | bytes 2162692
  32.5 16.9 %all-to-all-start.2 = ((bf16[4,2,16,2048]{3,2,1,0:T(8,128)(2,1)}), bf16[4,2,16,2048]{3,2,1,0:T(8,128)(2,1)S(1)}, u32[]{:S(2)}, u32[]{:S(2)}) async-start(bf16[4,2,16,2048]{3,2,1,0:T(8,128)(2,1)} %bitcast.19), calls=%async_computation.2 | async-start | bytes 1048576 | tf_op jit(solution)/shard_map/all_to_all | solution.py:166
  36.1 2.6 %copy-start.12 = (s32[1,8]{1,0:T(1,128)S(1)}, s32[1,8]{1,0:T(1,128)}, u32[]{:S(2)}) copy-start(s32[1,8]{1,0:T(1,128)} %param.23) | copy-start | bytes 100
  49.3 14.0 %all-to-all-start.1 = ((bf16[4,2,16,2048]{3,2,1,0:T(8,128)(2,1)}), bf16[4,2,16,2048]{3,2,1,0:T(8,128)(2,1)S(1)}, u32[]{:S(2)}, u32[]{:S(2)}) async-start(bf16[4,2,16,2048]{3,2,1,0:T(8,128)(2,1)} %bitcast.128), calls=%async_computation.1 | async-start | bytes 1048576 | tf_op jit(solution)/shard_map/all_to_all | solution.py:165
  67.0 5.3 %copy-start.2 = (f32[128,2048]{1,0:T(8,128)S(1)}, f32[128,2048]{1,0:T(8,128)}, u32[]{:S(2)}) copy-start(f32[128,2048]{1,0:T(8,128)} %convert_element_type.89) | copy-start | bytes 3145732
  67.0 5.3 %copy-start.9 = (f32[128,4]{1,0:T(8,128)S(1)}, f32[128,4]{1,0:T(8,128)}, u32[]{:S(2)}) copy-start(f32[128,4]{1,0:T(8,128)} %copy.40) | copy-start | bytes 6148
